TPU v7x, 32 devices: a whole 2x2x4 slice. The times are simulated.
32 devices in a mesh: dp: 8 (over z, y), expert: 4 (over x, core).
Axes of the slice: x: 2, y: 2, z: 4, core: 2. Of those that a mesh axis runs over, the one named last changes fastest.
Arguments:
- tokens: bfloat16 [8, 1024, 2048], P('dp', 'expert'), may hold values from -6 to 6
- cotangent: bfloat16 [8, 1024, 2048], P('dp', 'expert'), may hold values from -6 to 6
- attention_routes: int32 [8, 1024, 2], P('dp'), may hold values from 0 to 3, all different within a row; in each aligned block of 256 rows (0 to 255, 256 to 511, ..., all dimensions but the last counted through in order) at most 160 rows name the same one
- feedforward_routes: int32 [8, 1024, 2], P('dp'), may hold values from 0 to 3, all different within a row; in each aligned block of 256 rows (0 to 255, 256 to 511, ..., all dimensions but the last counted through in order) at most 160 rows name the same one
- prefix_length: int32 [8], P('dp'), may hold values from 102 to 512
- gain_attention: float32 [2048], replicated, may hold values from 0.25 to 1.75
- gain_feedforward: float32 [2048], replicated, may hold values from 0.25 to 1.75
- keyvalue_weight: bfloat16 [2048, 4096], P('dp'), may hold values from -0.125 to 0.125
- router_weight: bfloat16 [2048, 8], P('dp'), may hold values from -0.25 to 0.25
- query_weight: bfloat16 [4, 2048, 2048], P('expert', 'dp'), may hold values from -0.125 to 0.125
- output_weight: bfloat16 [4, 2048, 2048], P('expert', 'dp'), may hold values from -3 to 3
- gate_weight: bfloat16 [4, 5632, 2048], P('expert', 'dp'), may hold values from -0.125 to 0.125
- up_weight: bfloat16 [4, 5632, 2048], P('expert', 'dp'), may hold values from -0.125 to 0.125
- down_weight: bfloat16 [4, 5632, 2048], P('expert', 'dp'), may hold values from -0.15625 to 0.15625
Outputs:
- layer_output: bfloat16 [8, 1024, 2048], P('dp', 'expert')
- grad_tokens: float32 [8, 1024, 2048], P('dp', 'expert')
- grad_gain_attention: float32 [2048], P('dp')
- grad_gain_feedforward: float32 [2048], P('dp')
- grad_keyvalue: float32 [2048, 4096], P('dp')
- grad_router: float32 [2048, 8], P('dp')
- grad_query: float32 [4, 2048, 2048], P('expert', 'dp')
- grad_projection: float32 [4, 2048, 2048], P('expert', 'dp')
- grad_gate: float32 [4, 5632, 2048], P('expert', 'dp')
- grad_up: float32 [4, 5632, 2048], P('expert', 'dp')
- grad_down: float32 [4, 5632, 2048], P('expert', 'dp')
Inputs may be any that keep to these rules, and one draw needn't show every extreme that they name: `attention_routes`: the two ids of a token differ. Among the 256 tokens of one device (aligned blocks of each sequence) no expert is named more than 160 times, a bound that some block reaches. `feedforward_routes`: the two ids of a token differ. Among the 256 tokens of one device (aligned blocks of each sequence) no expert is named more than 160 times, a bound that some block reaches.
All inputs are finite; a program needn't handle non-finite values.
Results may differ from a plain program's by a relative error of at most 0.025.
Values may be sent and summed in bfloat16 or wider, within the bound.
A program may use at most 448 MiB of HBM per device.

v0:
```python
import jax
import jax.numpy as jnp
from jax import lax
from jax.sharding import PartitionSpec as P

HEADS = 16
HEAD_DIM = 128
EPS = 1e-06
NEG = -1e30
HIGH = lax.Precision.HIGHEST
ACROSS = (((1,), (1,)), ((), ()))
DOWNWARD = (((0,), (0,)), ((), ()))


def norm_parts(vector, gain_vector):
    factor = lax.rsqrt(jnp.mean(vector * vector, axis=-1, keepdims=True) + EPS)
    normed = vector * factor
    return (normed * gain_vector, normed, factor)


def norm_back(incoming, gain_vector, normed, factor):
    dnormed = incoming * gain_vector
    return factor * (dnormed - normed * jnp.mean(dnormed * normed, axis=-1, keepdims=True))


def route_plan(sequence_ids, my_index, group_size, tok_rows, slot_count):
    expert_range = jnp.arange(group_size, dtype=jnp.int32)
    matches_all = (sequence_ids[:, :, None] == expert_range[None, None, :]).astype(jnp.int32)
    chosen = jnp.sum(matches_all, axis=1).reshape(group_size, tok_rows, group_size)
    ranking = jnp.cumsum(chosen, axis=1) - chosen
    slot_ids = jnp.arange(slot_count, dtype=jnp.int32)[None, :, None]
    block_pick = (expert_range == my_index).astype(jnp.int32)
    my_chosen = jnp.sum(chosen * block_pick[:, None, None], axis=0).T
    my_ranking = jnp.sum(ranking * block_pick[:, None, None], axis=0).T
    send_table = (
        my_chosen[:, None, :] * (my_ranking[:, None, :] == slot_ids).astype(jnp.int32)
    ).astype(jnp.float32)
    column_chosen = jnp.sum(chosen * block_pick[None, None, :], axis=2)
    column_ranking = jnp.sum(ranking * block_pick[None, None, :], axis=2)
    taken = column_chosen[:, None, :] * (column_ranking[:, None, :] == slot_ids).astype(jnp.int32)
    positions = (
        expert_range[:, None, None] * tok_rows
        + jnp.arange(tok_rows, dtype=jnp.int32)[None, None, :]
    )
    arrival_places = jnp.sum(taken * positions, axis=2).reshape(-1)
    my_ids = lax.dynamic_slice_in_dim(sequence_ids, my_index * tok_rows, tok_rows, 0)
    matches = (my_ids[:, :, None] == expert_range[None, None, :]).astype(jnp.float32)
    return (send_table, arrival_places, matches)


def pair_gates(logits, matches):
    selected = jnp.sum(matches * logits[:, None, :], axis=2)
    largest = jnp.max(selected, axis=1, keepdims=True)
    exponent = jnp.exp(selected - largest)
    weights = exponent / jnp.sum(exponent, axis=1, keepdims=True)
    return (weights, jnp.sum(weights[:, :, None] * matches, axis=1))


def gates_back(dgate, weights, matches):
    dweights = jnp.sum(dgate[:, None, :] * matches, axis=2)
    dselected = weights * (dweights - jnp.sum(weights * dweights, axis=1, keepdims=True))
    return jnp.sum(dselected[:, :, None] * matches, axis=1)


def merge_back(send_table, gate_table, returned):
    weighted = send_table * gate_table.T[:, None, :]
    return jnp.einsum("ect,ecd->td", weighted, returned.astype(jnp.float32), precision=HIGH)


def branch_cotangent(send_table, gate_table, returned, incoming):
    spread_grad = jnp.einsum("ect,td->ecd", send_table, incoming, precision=HIGH)
    slot_gate = jnp.sum(send_table * gate_table.T[:, None, :], axis=2)
    cotangent_rows = (spread_grad * slot_gate[:, :, None]).astype(jnp.bfloat16)
    slot_dgate = jnp.sum(spread_grad * returned.astype(jnp.float32), axis=2)
    dgate = jnp.einsum("ect,ec->te", send_table, slot_dgate, precision=HIGH)
    return (cotangent_rows, dgate)


def dispatch(rows):
    return lax.all_to_all(rows, "expert", split_axis=0, concat_axis=0, tiled=True)


def collect(rows):
    return lax.all_to_all(rows, "expert", split_axis=0, concat_axis=0, tiled=True)


def spread_rows(rows):
    return lax.all_gather(rows, "dp", axis=0, tiled=True)


def sum_rows(terms):
    return lax.psum_scatter(
        terms.astype(jnp.bfloat16), "dp", scatter_dimension=0, tiled=True
    ).astype(jnp.float32)


def send_rows(send_table, rows):
    return jnp.einsum(
        "ect,td->ecd", send_table.astype(jnp.bfloat16), rows, preferred_element_type=jnp.float32
    ).astype(jnp.bfloat16)


def per_device(
    tokens,
    cotangent,
    attention_routes,
    feedforward_routes,
    prefix_length,
    gain_attention,
    gain_feedforward,
    keyvalue_weight,
    router_weight,
    query_weight,
    output_weight,
    gate_weight,
    up_weight,
    down_weight,
):
    my_index = lax.axis_index("expert")
    group_size = lax.axis_size("expert")
    inputs = tokens[0].astype(jnp.float32)
    tok_rows = inputs.shape[0]
    model_width = inputs.shape[1]
    seq_total = tok_rows * group_size
    slot_count = 5 * 2 * tok_rows // (4 * group_size)
    query_width = HEADS * HEAD_DIM
    scaling = HEAD_DIM ** (-0.5)
    keyvalue_full, router_full, query_full, output_full = (
        lax.all_gather(keyvalue_weight, "dp", axis=0, tiled=True),
        lax.all_gather(router_weight, "dp", axis=0, tiled=True),
        lax.all_gather(query_weight[0], "dp", axis=0, tiled=True),
        lax.all_gather(output_weight[0], "dp", axis=0, tiled=True),
    )
    attention_cols = router_full[:, :group_size]
    feedforward_cols = router_full[:, group_size:]
    normed_attention, unit_attention, factor_attention = norm_parts(inputs, gain_attention)
    attention_in = normed_attention.astype(jnp.bfloat16)
    keyvalue_rows = jnp.dot(attention_in, keyvalue_full, preferred_element_type=jnp.float32).astype(
        jnp.bfloat16
    )
    keyvalue_seq = lax.all_gather(keyvalue_rows, "expert", axis=0, tiled=True)
    key_rows = keyvalue_seq[:, :query_width].reshape(seq_total, HEADS, HEAD_DIM)
    value_rows = keyvalue_seq[:, query_width:].reshape(seq_total, HEADS, HEAD_DIM)
    attend_table, attend_places, attend_matches = route_plan(
        attention_routes[0], my_index, group_size, tok_rows, slot_count
    )
    attend_logits = jnp.dot(attention_in, attention_cols, preferred_element_type=jnp.float32)
    attend_weights, attend_gate = pair_gates(attend_logits, attend_matches)
    arrived = dispatch(send_rows(attend_table, attention_in)).reshape(-1, model_width)
    queries = jnp.dot(arrived, query_full, preferred_element_type=jnp.float32).astype(jnp.bfloat16)
    queries = queries.reshape(-1, HEADS, HEAD_DIM)
    key_places = jnp.arange(seq_total, dtype=jnp.int32)
    allowed = (key_places[None, :] <= attend_places[:, None]) | (
        key_places[None, :] < prefix_length[0]
    )
    scores = (
        jnp.einsum("rhd,khd->hrk", queries, key_rows, preferred_element_type=jnp.float32) * scaling
    )
    scores = jnp.where(allowed[None], scores, NEG)
    row_max = jnp.max(scores, axis=2, keepdims=True)
    exponent = jnp.exp(scores - row_max)
    row_total = jnp.sum(exponent, axis=2, keepdims=True)
    log_total = row_max + jnp.log(row_total)
    attention_low = (exponent / row_total).astype(jnp.bfloat16)
    mixture = jnp.einsum(
        "hrk,khd->rhd", attention_low, value_rows, preferred_element_type=jnp.float32
    )
    mixture = mixture.astype(jnp.bfloat16).reshape(-1, query_width)
    attend_branch = jnp.dot(mixture, output_full, preferred_element_type=jnp.float32).astype(
        jnp.bfloat16
    )
    attend_returned = collect(attend_branch.reshape(group_size, slot_count, model_width))
    hidden = inputs + merge_back(attend_table, attend_gate, attend_returned)
    normed_feed, unit_feed, factor_feed = norm_parts(hidden, gain_feedforward)
    feed_in = normed_feed.astype(jnp.bfloat16)
    feed_table, _, feed_matches = route_plan(
        feedforward_routes[0], my_index, group_size, tok_rows, slot_count
    )
    feed_logits = jnp.dot(feed_in, feedforward_cols, preferred_element_type=jnp.float32)
    feed_weights, feed_gate = pair_gates(feed_logits, feed_matches)
    feed_rows = dispatch(send_rows(feed_table, feed_in)).reshape(-1, model_width)
    everyone = spread_rows(feed_rows)
    pre_gate = lax.dot_general(everyone, gate_weight[0], ACROSS, preferred_element_type=jnp.float32)
    pre_up = lax.dot_general(everyone, up_weight[0], ACROSS, preferred_element_type=jnp.float32)
    act_low = (pre_gate * jax.nn.sigmoid(pre_gate) * pre_up).astype(jnp.bfloat16)
    feed_branch = sum_rows(
        jnp.dot(act_low, down_weight[0], preferred_element_type=jnp.float32)
    ).astype(jnp.bfloat16)
    feed_returned = collect(feed_branch.reshape(group_size, slot_count, model_width))
    layer_output = hidden + merge_back(feed_table, feed_gate, feed_returned)
    gradient = cotangent[0].astype(jnp.float32)
    feed_cot, feed_dgate = branch_cotangent(feed_table, feed_gate, feed_returned, gradient)
    feed_dlogits = gates_back(feed_dgate, feed_weights, feed_matches)
    feed_cot_rows = dispatch(feed_cot).reshape(-1, model_width)
    cot_everyone = spread_rows(feed_cot_rows)
    sigmoid_gate = jax.nn.sigmoid(pre_gate)
    act_grad = lax.dot_general(
        cot_everyone, down_weight[0], ACROSS, preferred_element_type=jnp.float32
    )
    dgate_low = (act_grad * pre_up * sigmoid_gate * (1.0 + pre_gate * (1.0 - sigmoid_gate))).astype(
        jnp.bfloat16
    )
    dup_low = (act_grad * pre_gate * sigmoid_gate).astype(jnp.bfloat16)
    grad_gate = lax.dot_general(dgate_low, everyone, DOWNWARD, preferred_element_type=jnp.float32)
    grad_up = lax.dot_general(dup_low, everyone, DOWNWARD, preferred_element_type=jnp.float32)
    grad_down = lax.dot_general(act_low, cot_everyone, DOWNWARD, preferred_element_type=jnp.float32)
    feed_dx = sum_rows(
        jnp.dot(dgate_low, gate_weight[0], preferred_element_type=jnp.float32)
        + jnp.dot(dup_low, up_weight[0], preferred_element_type=jnp.float32)
    )
    feed_home = lax.all_to_all(
        feed_dx.reshape(group_size, slot_count, model_width).astype(jnp.bfloat16),
        "expert",
        split_axis=0,
        concat_axis=0,
        tiled=True,
    ).astype(jnp.float32)
    feed_dnorm = jnp.einsum("ect,ecd->td", feed_table, feed_home, precision=HIGH) + jnp.dot(
        feed_dlogits, feedforward_cols.astype(jnp.float32).T, precision=HIGH
    )
    grad_gain_feed = jnp.sum(feed_dnorm * unit_feed, axis=0)
    hidden_grad = gradient + norm_back(feed_dnorm, gain_feedforward, unit_feed, factor_feed)
    attend_cot, attend_dgate = branch_cotangent(
        attend_table, attend_gate, attend_returned, hidden_grad
    )
    attend_dlogits = gates_back(attend_dgate, attend_weights, attend_matches)
    attend_cot_rows = dispatch(attend_cot).reshape(-1, model_width)
    dmixture = lax.dot_general(
        attend_cot_rows, output_full, ACROSS, preferred_element_type=jnp.float32
    )
    dmixture = dmixture.astype(jnp.bfloat16).reshape(-1, HEADS, HEAD_DIM)
    grad_projection = lax.dot_general(
        mixture, attend_cot_rows, DOWNWARD, preferred_element_type=jnp.float32
    )
    scores_again = (
        jnp.einsum("rhd,khd->hrk", queries, key_rows, preferred_element_type=jnp.float32) * scaling
    )
    attention = jnp.where(allowed[None], jnp.exp(scores_again - log_total), 0.0)
    attention_again = attention.astype(jnp.bfloat16)
    dattention = jnp.einsum(
        "rhd,khd->hrk", dmixture, value_rows, preferred_element_type=jnp.float32
    )
    row_dot = jnp.sum(attention * dattention, axis=2, keepdims=True)
    dscores = (attention * (dattention - row_dot)).astype(jnp.bfloat16)
    dqueries = (
        jnp.einsum("hrk,khd->rhd", dscores, key_rows, preferred_element_type=jnp.float32) * scaling
    )
    dqueries = dqueries.astype(jnp.bfloat16).reshape(-1, query_width)
    dkeys = (
        jnp.einsum("hrk,rhd->khd", dscores, queries, preferred_element_type=jnp.float32) * scaling
    )
    dvalues = jnp.einsum(
        "hrk,rhd->khd", attention_again, dmixture, preferred_element_type=jnp.float32
    )
    grad_query = lax.dot_general(arrived, dqueries, DOWNWARD, preferred_element_type=jnp.float32)
    attend_dx = lax.dot_general(dqueries, query_full, ACROSS, preferred_element_type=jnp.float32)
    keyvalue_terms = jnp.concatenate(
        [dkeys.reshape(seq_total, query_width), dvalues.reshape(seq_total, query_width)], axis=1
    ).reshape(group_size, tok_rows, 2 * query_width)
    attend_home, keyvalue_home = (
        lax.all_to_all(
            attend_dx.reshape(group_size, slot_count, model_width).astype(jnp.bfloat16),
            "expert",
            split_axis=0,
            concat_axis=0,
            tiled=True,
        ).astype(jnp.float32),
        lax.all_to_all(
            keyvalue_terms.astype(jnp.bfloat16), "expert", split_axis=0, concat_axis=0, tiled=True
        ).astype(keyvalue_terms.dtype),
    )
    dkeyvalue = jnp.sum(keyvalue_home, axis=0).astype(jnp.bfloat16)
    attend_dnorm = (
        jnp.einsum("ect,ecd->td", attend_table, attend_home, precision=HIGH)
        + lax.dot_general(dkeyvalue, keyvalue_full, ACROSS, preferred_element_type=jnp.float32)
        + jnp.dot(attend_dlogits, attention_cols.astype(jnp.float32).T, precision=HIGH)
    )
    grad_keyvalue = lax.dot_general(
        attention_in, dkeyvalue, DOWNWARD, preferred_element_type=jnp.float32
    )
    grad_router = jnp.concatenate(
        [
            jnp.dot(attention_in.astype(jnp.float32).T, attend_dlogits, precision=HIGH),
            jnp.dot(feed_in.astype(jnp.float32).T, feed_dlogits, precision=HIGH),
        ],
        axis=1,
    )
    grad_gain_attend = jnp.sum(attend_dnorm * unit_attention, axis=0)
    grad_tokens = hidden_grad + norm_back(
        attend_dnorm, gain_attention, unit_attention, factor_attention
    )
    reduced = (
        lax.psum_scatter(
            grad_keyvalue.astype(jnp.bfloat16), "dp", scatter_dimension=0, tiled=True
        ).astype(jnp.float32),
        lax.psum_scatter(
            grad_router.astype(jnp.bfloat16), "dp", scatter_dimension=0, tiled=True
        ).astype(jnp.float32),
        lax.psum_scatter(
            grad_query.astype(jnp.bfloat16), "dp", scatter_dimension=0, tiled=True
        ).astype(jnp.float32),
        lax.psum_scatter(
            grad_projection.astype(jnp.bfloat16), "dp", scatter_dimension=0, tiled=True
        ).astype(jnp.float32),
        lax.psum_scatter(
            grad_gain_attend.astype(jnp.bfloat16), "dp", scatter_dimension=0, tiled=True
        ).astype(jnp.float32),
        lax.psum_scatter(
            grad_gain_feed.astype(jnp.bfloat16), "dp", scatter_dimension=0, tiled=True
        ).astype(jnp.float32),
    )
    shared = (
        lax.psum(reduced[0].astype(jnp.bfloat16), "expert").astype(jnp.float32),
        lax.psum(reduced[1].astype(jnp.bfloat16), "expert").astype(jnp.float32),
        lax.psum(reduced[4].astype(jnp.bfloat16), "expert").astype(jnp.float32),
        lax.psum(reduced[5].astype(jnp.bfloat16), "expert").astype(jnp.float32),
    )
    return (
        layer_output.astype(jnp.bfloat16)[None],
        grad_tokens[None],
        shared[2],
        shared[3],
        shared[0],
        shared[1],
        reduced[2][None],
        reduced[3][None],
        grad_gate[None],
        grad_up[None],
        grad_down[None],
    )


def solution(mesh):
    in_specs = (
        P("dp", "expert", None),
        P("dp", "expert", None),
        P("dp", None, None),
        P("dp", None, None),
        P("dp"),
        P(),
        P(),
        P("dp", None),
        P("dp", None),
        P("expert", "dp", None),
        P("expert", "dp", None),
        P("expert", "dp", None),
        P("expert", "dp", None),
        P("expert", "dp", None),
    )
    out_specs = (
        P("dp", "expert", None),
        P("dp", "expert", None),
        P("dp"),
        P("dp"),
        P("dp", None),
        P("dp", None),
        P("expert", "dp", None),
        P("expert", "dp", None),
        P("expert", "dp", None),
        P("expert", "dp", None),
        P("expert", "dp", None),
    )
    return jax.shard_map(
        per_device, mesh=mesh, in_specs=in_specs, out_specs=out_specs, check_vma=False
    )
```

profile of v0, /device:TPU:0, one launch (start us, length us, event | category | flops | bytes accessed | tf_op | source)
XLA Modules:
  0.0 3382.4 jit_solution(1048255030446471202)
XLA Ops:
  10.3 230.2 %all-gather.9.cloned.1.call-done = bf16[2048,4096]{1,0:T(8,128)(2,1)} async-done(((bf16[256,4096]{1,0:T(8,128)(2,1)}), bf16[2048,4096]{1,0:T(8,128)(2,1)}) %all-gather.9.cloned.1.call-update) | async-done | bytes 16777232 | tf_op jit(solution)/shard_map/all_gather | solution.py:129
  303.1 62.6 %all-gather.17.cloned.1.call-done = bf16[1,2048,2048]{2,1,0:T(8,128)(2,1)} async-done(((bf16[1,256,2048]{2,1,0:T(8,128)(2,1)}), bf16[1,2048,2048]{2,1,0:T(8,128)(2,1)}) %all-gather.17.cloned.1.call-update) | async-done | bytes 8388624 | tf_op jit(solution)/shard_map/all_gather | solution.py:131
  381.0 43.4 %all-gather.11.cloned.1.call-done = bf16[1024,4096]{1,0:T(8,128)(2,1)} async-done(((bf16[256,4096]{1,0:T(8,128)(2,1)}), bf16[1024,4096]{1,0:T(8,128)(2,1)}) %all-gather.11.cloned.1.call-update) | async-done | bytes 8388624 | tf_op jit(solution)/shard_map/all_gather | solution.py:141
  498.4 53.0 %all-gather.19.cloned.1.call-done = bf16[1,2048,2048]{2,1,0:T(8,128)(2,1)} async-done(((bf16[1,256,2048]{2,1,0:T(8,128)(2,1)}), bf16[1,2048,2048]{2,1,0:T(8,128)(2,1)}) %all-gather.19.cloned.1.call-update) | async-done | bytes 8388624 | tf_op jit(solution)/shard_map/all_gather | solution.py:132
  566.1 30.4 all_gather.21
  606.4 34.6 %all_to_all.45 = bf16[4,160,2048]{2,1,0:T(8,128)(2,1)} all-to-all(bf16[4,160,2048]{2,1,0:T(8,128)(2,1)S(1)} %convolution_convert_fusion.5), channel_id=1, replica_groups=mesh['dp'=8,'expert'=4] {'expert'}, dimensions={0} | all-to-all | bytes 5242880 | tf_op jit(solution)/shard_map/all_to_all | solution.py:80
  641.1 399.0 %all-gather.13.cloned.1.call-done = bf16[5120,2048]{1,0:T(8,128)(2,1)} async-done(((bf16[640,2048]{1,0:T(8,128)(2,1)}), bf16[5120,2048]{1,0:T(8,128)(2,1)}) %all-gather.13.cloned.1.call-update) | async-done | bytes 20971536 | tf_op jit(solution)/shard_map/all_gather | solution.py:88
  1062.5 29.8 multiply_convert_fusion.3
  1115.6 343.6 %reduce-scatter.7.cloned.1.call-done = bf16[640,2048]{1,0:T(8,128)(2,1)} async-done(((bf16[5120,2048]{1,0:T(8,128)(2,1)}), bf16[640,2048]{1,0:T(8,128)(2,1)}) %reduce-scatter.7.cloned.1.call-update) | async-done | bytes 2621456 | tf_op jit(solution)/shard_map/reduce_scatter | solution.py:92
  1466.1 29.0 all-to-all-done.3
  1505.8 34.6 %all_to_all.46 = bf16[4,160,2048]{2,1,0:T(8,128)(2,1)} all-to-all(bf16[4,160,2048]{2,1,0:T(8,128)(2,1)S(1)} %multiply_convert_fusion.7), channel_id=1, replica_groups=mesh['dp'=8,'expert'=4] {'expert'}, dimensions={0} | all-to-all | bytes 5242880 | tf_op jit(solution)/shard_map/all_to_all | solution.py:80
  1540.4 400.1 %all-gather.15.cloned.1.call-done = bf16[5120,2048]{1,0:T(8,128)(2,1)} async-done(((bf16[640,2048]{1,0:T(8,128)(2,1)}), bf16[5120,2048]{1,0:T(8,128)(2,1)}) %all-gather.15.cloned.1.call-update) | async-done | bytes 20971536 | tf_op jit(solution)/shard_map/all_gather | solution.py:88
  1940.6 42.0 %multiply_convert_fusion.1 = (bf16[5120,704]{0,1:T(8,128)(2,1)}, bf16[5120,704]{0,1:T(8,128)(2,1)}) fusion(f32[5120,704]{0,1:T(8,128)} %fusion.44, f32[5120,704]{0,1:T(8,128)} %get-tuple-element.45, bf16[5120,2048]{1,0:T(8,128)(2,1)} %all-gather.15.cloned.1.call-done, bf16[1,704,2048]{2,1,0:T(8,128)(2,1)S(1)} %copy-done), kind=kOutput, calls=%fused_computation.14 | convolution fusion | flops 14810808320 | bytes 67108864 | tf_op jit(solution)/shard_map/dot_general | solution.py:197
  2009.7 28.7 add_convert_fusion
  2038.4 343.6 %reduce-scatter.9.cloned.1.call-done = bf16[640,2048]{1,0:T(8,128)(2,1)} async-done(((bf16[5120,2048]{1,0:T(8,128)(2,1)}), bf16[640,2048]{1,0:T(8,128)(2,1)}) %reduce-scatter.9.cloned.1.call-update) | async-done | bytes 2621456 | tf_op jit(solution)/shard_map/reduce_scatter | solution.py:92
  2387.1 31.1 all-to-all-done.5
  2438.2 31.2 all-to-all-done.6
  2502.5 35.8 %multiply_reduce_fusion = (f32[16,640]{1,0:T(8,128)S(1)}, f32[16,640,1024]{2,1,0:T(8,128)}) fusion(f32[16,640,1024]{2,1,0:T(8,128)} %get-tuple-element.41, f32[16,640]{1,0:T(8,128)S(1)} %log_add_fusion, pred[640,1024]{1,0:T(8,128)(4,1)S(1)} %copy-done.7, bf16[640,16,128]{0,2,1:T(8,128)(2,1)S(1)} %bitcast.245, bf16[128,16,8,128]{3,2,1,0:T(8,128)(2,1)} %get-tuple-element.36), kind=kOutput, calls=%fused_computation.1 | convolution fusion | flops 2736773120 | bytes 91439104 | tf_op jit(solution)/shard_map/rhd,khd->hrk/dot_general | solution.py:240
  2550.8 34.3 %multiply_convert_fusion = bf16[16,640,1024]{2,1,0:T(8,128)(2,1)} fusion(f32[16,640,1024]{2,1,0:T(8,128)} %get-tuple-element.50, f32[16,640,1024]{2,1,0:T(8,128)} %get-tuple-element.41, f32[16,640]{1,0:T(8,128)S(1)} %get-tuple-element.49, f32[16,640]{1,0:T(8,128)S(1)} %log_add_fusion, pred[640,1024]{1,0:T(8,128)(4,1)S(1)} %copy-done.7), kind=kLoop, calls=%fused_computation | loop fusion | flops 62914560 | bytes 105594880 | tf_op jit(solution)/shard_map/convert_element_type | solution.py:244
  2625.9 90.6 %all-to-all-done.8 = bf16[4,256,4096]{1,2,0:T(8,128)(2,1)} async-done(((bf16[4,256,4096]{1,2,0:T(8,128)(2,1)}), bf16[4,256,4096]{1,2,0:T(8,128)(2,1)}, u32[]{:S(2)}, u32[]{:S(2)}) %all-to-all-start.8) | async-done | bytes 8388640 | tf_op jit(solution)/shard_map/all_to_all | solution.py:268
  2931.0 84.0 %reduce-scatter.11.cloned.1.call-done = bf16[256,4096]{1,0:T(8,128)(2,1)} async-done(((bf16[2048,4096]{1,0:T(8,128)(2,1)}), bf16[256,4096]{1,0:T(8,128)(2,1)}) %reduce-scatter.11.cloned.1.call-update) | async-done | bytes 2097168 | tf_op jit(solution)/shard_map/reduce_scatter | solution.py:293
  3015.0 152.1 %reduce-scatter.17.cloned.1.call-done = bf16[256,2048]{1,0:T(8,128)(2,1)} async-done(((bf16[2048,2048]{1,0:T(8,128)(2,1)}), bf16[256,2048]{1,0:T(8,128)(2,1)}) %reduce-scatter.17.cloned.1.call-update) | async-done | bytes 1048592 | tf_op jit(solution)/shard_map/reduce_scatter | solution.py:302
  3170.1 148.6 %reduce-scatter.15.cloned.1.call-done = bf16[256,2048]{1,0:T(8,128)(2,1)} async-done(((bf16[2048,2048]{1,0:T(8,128)(2,1)}), bf16[256,2048]{1,0:T(8,128)(2,1)}) %reduce-scatter.15.cloned.1.call-update) | async-done | bytes 1048592 | tf_op jit(solution)/shard_map/reduce_scatter | solution.py:299
  3321.5 50.1 %all-reduce.6.cloned.1.call-done = bf16[256,4096]{1,0:T(8,128)(2,1)} async-done(((bf16[256,4096]{1,0:T(8,128)(2,1)}), bf16[256,4096]{1,0:T(8,128)(2,1)}) %all-reduce.6.cloned.1.call-update) | async-done | bytes 2097168 | tf_op jit(solution)/shard_map/psum | solution.py:313
  (314 shorter events, 603.6 us)
Async XLA Ops:
  7.2 1085.2 %copy-start = (bf16[1,704,2048]{2,1,0:T(8,128)(2,1)S(1)}, bf16[1,704,2048]{2,1,0:T(8,128)(2,1)}, u32[]{:S(2)}) copy-start(bf16[1,704,2048]{2,1,0:T(8,128)(2,1)} %param.27) | copy-start | bytes 8650756
  7.2 233.3 %all-gather.9.cloned.1.call-start = ((), (), s32[]{:S(2)}) async-start(), calls=%async_computation.15 | async-start | bytes 18874368 | tf_op jit(solution)/shard_map/all_gather | solution.py:129
  7.9 357.8 %all-gather.17.cloned.1.call-start = ((), (), s32[]{:S(2)}) async-start(), calls=%async_computation.26 | async-start | bytes 9437184 | tf_op jit(solution)/shard_map/all_gather | solution.py:131
  8.7 415.7 %all-gather.11.cloned.1.call-start = ((), (), s32[]{:S(2)}) async-start(), calls=%async_computation.16 | async-start | bytes 10485760 | tf_op jit(solution)/shard_map/all_gather | solution.py:141
  263.4 2154.8 %copy-start.23 = (s32[256,4]{0,1:T(4,128)}, s32[256,4]{0,1:T(4,128)S(1)}, u32[]{:S(2)}) copy-start(s32[256,4]{0,1:T(4,128)S(1)} %get-tuple-element.17) | copy-start | bytes 12292
  263.4 2154.8 %copy-start.25 = (s32[256,4]{0,1:T(4,128)}, s32[256,4]{0,1:T(4,128)S(1)}, u32[]{:S(2)}) copy-start(s32[256,4]{0,1:T(4,128)S(1)} %get-tuple-element.18) | copy-start | bytes 12292
  267.2 35.9 %all-to-all-start = ((bf16[4,160,2048]{2,1,0:T(8,128)(2,1)}), bf16[4,160,2048]{2,1,0:T(8,128)(2,1)}, u32[]{:S(2)}, u32[]{:S(2)}) async-start(bf16[4,160,2048]{2,1,0:T(8,128)(2,1)} %convolution_convert_fusion.6), calls=%async_computation | async-start | bytes 5242880 | tf_op jit(solution)/shard_map/all_to_all | solution.py:80
  271.7 279.6 %all-gather.19.cloned.1.call-start = ((), (), s32[]{:S(2)}) async-start(), calls=%async_computation.27 | async-start | bytes 9437184 | tf_op jit(solution)/shard_map/all_gather | solution.py:132
  561.3 37.8 %all-to-all-start.1 = ((bf16[4,160,2048]{2,1,0:T(8,128)(2,1)}), bf16[4,160,2048]{2,1,0:T(8,128)(2,1)}, u32[]{:S(2)}, u32[]{:S(2)}) async-start(bf16[4,160,2048]{2,1,0:T(8,128)(2,1)} %bitcast.250), calls=%async_computation.1 | async-start | bytes 5242880 | tf_op jit(solution)/shard_map/all_to_all | solution.py:84
  566.0 474.0 %all-gather.13.cloned.1.call-start = ((), (), s32[]{:S(2)}) async-start(), calls=%async_computation.17 | async-start | bytes 23592960 | tf_op jit(solution)/shard_map/all_gather | solution.py:88
  596.5 1826.1 %copy-start.17 = (bf16[2048,8]{0,1:T(8,128)(2,1)}, bf16[2048,8]{0,1:T(8,128)(2,1)S(1)}, u32[]{:S(2)}) copy-start(bf16[2048,8]{0,1:T(8,128)(2,1)S(1)} %all_gather.21) | copy-start | bytes 98308
  641.0 818.1 %reduce-scatter.7.cloned.1.call-start = ((), (), s32[]{:S(2)}) async-start(), calls=%async_computation.18 | async-start | bytes 23592960 | tf_op jit(solution)/shard_map/reduce_scatter | solution.py:92
  1459.2 36.0 %all-to-all-start.3 = ((bf16[4,160,2048]{2,1,0:T(8,128)(2,1)}), bf16[4,160,2048]{2,1,0:T(8,128)(2,1)}, u32[]{:S(2)}, u32[]{:S(2)}) async-start(bf16[4,160,2048]{2,1,0:T(8,128)(2,1)} %bitcast.251), calls=%async_computation.4 | async-start | bytes 5242880 | tf_op jit(solution)/shard_map/all_to_all | solution.py:84
  1463.8 476.8 %all-gather.15.cloned.1.call-start = ((), (), s32[]{:S(2)}) async-start(), calls=%async_computation.19 | async-start | bytes 23592960 | tf_op jit(solution)/shard_map/all_gather | solution.py:88
  1540.4 841.5 %reduce-scatter.9.cloned.1.call-start = ((), (), s32[]{:S(2)}) async-start(), calls=%async_computation.20 | async-start | bytes 23592960 | tf_op jit(solution)/shard_map/reduce_scatter | solution.py:92
  2381.9 36.3 %all-to-all-start.5 = ((bf16[4,160,2048]{2,1,0:T(8,128)(2,1)}), bf16[4,160,2048]{2,1,0:T(8,128)(2,1)}, u32[]{:S(2)}, u32[]{:S(2)}) async-start(bf16[4,160,2048]{2,1,0:T(8,128)(2,1)} %bitcast.252), calls=%async_computation.7 | async-start | bytes 5242880 | tf_op jit(solution)/shard_map/all_to_all | solution.py:211
  2434.0 35.5 %all-to-all-start.6 = ((bf16[4,160,2048]{2,1,0:T(8,128)(2,1)}), bf16[4,160,2048]{2,1,0:T(8,128)(2,1)S(1)}, u32[]{:S(2)}, u32[]{:S(2)}) async-start(bf16[4,160,2048]{2,1,0:T(8,128)(2,1)} %get-tuple-element.39), calls=%async_computation.8 | async-start | bytes 5242880 | tf_op jit(solution)/shard_map/all_to_all | solution.py:80
  2617.5 99.0 %all-to-all-start.8 = ((bf16[4,256,4096]{1,2,0:T(8,128)(2,1)}), bf16[4,256,4096]{1,2,0:T(8,128)(2,1)}, u32[]{:S(2)}, u32[]{:S(2)}) async-start(bf16[4,256,4096]{1,2,0:T(8,128)(2,1)} %pad_maximum_fusion), calls=%async_computation.10 | async-start | bytes 16777216 | tf_op jit(solution)/shard_map/all_to_all | solution.py:268
  2623.3 294.5 %reduce-scatter.13.cloned.1.call-start = ((), (), s32[]{:S(2)}) async-start(), calls=%async_computation.23 | async-start | bytes 36864 | tf_op jit(solution)/shard_map/reduce_scatter | solution.py:296
  2625.8 389.2 %reduce-scatter.11.cloned.1.call-start = ((), (), s32[]{:S(2)}) async-start(), calls=%async_computation.21 | async-start | bytes 18874368 | tf_op jit(solution)/shard_map/reduce_scatter | solution.py:293
  2732.9 434.2 %reduce-scatter.17.cloned.1.call-start = ((), (), s32[]{:S(2)}) async-start(), calls=%async_computation.25 | async-start | bytes 9437184 | tf_op jit(solution)/shard_map/reduce_scatter | solution.py:302
  2745.6 573.1 %reduce-scatter.15.cloned.1.call-start = ((), (), s32[]{:S(2)}) async-start(), calls=%async_computation.24 | async-start | bytes 9437184 | tf_op jit(solution)/shard_map/reduce_scatter | solution.py:299
  2837.9 35.9 %all-to-all-start.7 = ((bf16[4,160,2048]{2,1,0:T(8,128)(2,1)}), bf16[4,160,2048]{2,1,0:T(8,128)(2,1)}, u32[]{:S(2)}, u32[]{:S(2)}) async-start(bf16[4,160,2048]{2,1,0:T(8,128)(2,1)} %fusion.26), calls=%async_computation.9 | async-start | bytes 5242880 | tf_op jit(solution)/shard_map/all_to_all | solution.py:261
  2842.5 529.1 %all-reduce.6.cloned.1.call-start = ((), (), s32[]{:S(2)}) async-start(), calls=%async_computation.22 | async-start | bytes 4194304 | tf_op jit(solution)/shard_map/psum | solution.py:313
  (73 other events, 3552.8 us)
Sparse Core Ops, SparseCore 0:
  10.2 230.2 all-gather.8
  242.6 123.0 all-gather.16
  367.9 56.4 all-gather.10
  426.4 124.9 all-gather.18
  641.2 398.8 all-gather.12
  1115.8 343.3 reduce-scatter.6
  1540.5 400.0 all-gather.14
  2038.5 343.4 reduce-scatter.8
  2627.2 53.1 reduce-scatter.12
  2733.0 281.9 reduce-scatter.10
  3019.1 148.0 reduce-scatter.16
  3170.6 148.0 reduce-scatter.14
  3321.2 50.3 all-reduce.5
where the time goes:
time: 3390 us; the launch traced here: 3380 us
  waiting for transfers between devices  2530 us (75%)
  matrix products  506 us (15%)
  blocking collectives  126 us (4%)
  other arithmetic  101 us (3%)
  local copies, waits for them, and re-layouts  66.8 us (2%)
  starting transfers between devices  34.3 us (1%)
    all_gather x2, waiting for transfers between devices, spread_rows(): return lax.all_gather(rows, 'dp', axis=0, tiled=True)  799 us
    reduce_scatter x2, waiting for transfers between devices, sum_rows(): lax.psum_scatter(terms.astype(jnp.bfloat16), 'dp', scatter_dimension=0, t...  687 us
    all_gather x1, waiting for transfers between devices, per_device(): lax.all_gather(keyvalue_weight, 'dp', axis=0, tiled=True)  230 us
    reduce_scatter x1, waiting for transfers between devices, per_device(): lax.psum_scatter(grad_projection.astype(jnp.bfloat16), 'dp', scatter_dime...  152 us
    reduce_scatter x1, waiting for transfers between devices, per_device(): lax.psum_scatter(grad_query.astype(jnp.bfloat16), 'dp', scatter_dimension...  149 us
    all_to_all x1, waiting for transfers between devices, per_device(): lax.all_to_all(keyvalue_terms.astype(jnp.bfloat16), 'expert', split_axis=...  90.6 us
    reduce_scatter x1, waiting for transfers between devices, per_device(): lax.psum_scatter(grad_keyvalue.astype(jnp.bfloat16), 'dp', scatter_dimens...  84 us
    all_to_all x2, blocking collectives, dispatch(): lax.all_to_all(rows, 'expert', split_axis=0, concat_axis=0, tiled=True)  69.2 us
  transfers between devices with their start and end apart: 20, of which 18 were waited for; matrix products, arithmetic and copies ran while one was open for 9% of the time, Pallas kernels for 0%

commit v1 on v0

--- a/solution.py
+++ b/solution.py
@@ -10,6 +10,18 @@
 HIGH = lax.Precision.HIGHEST
 ACROSS = (((1,), (1,)), ((), ()))
 DOWNWARD = (((0,), (0,)), ((), ()))
+
+
+def collect_2(array, axis, dim):
+    ways, here = (lax.axis_size(axis), lax.axis_index(axis))
+    grown, reach = (array, 1)
+    while reach < ways:
+        theirs = lax.ppermute(grown, axis, [(d, d ^ reach) for d in range(ways)])
+        mine_first = jnp.concatenate([grown, theirs], axis=dim)
+        theirs_first = jnp.concatenate([theirs, grown], axis=dim)
+        grown = jnp.where(here & reach == 0, mine_first, theirs_first)
+        reach = 2 * reach
+    return grown
 
 
 def norm_parts(vector, gain_vector):
@@ -85,7 +97,7 @@
 
 
 def spread_rows(rows):
-    return lax.all_gather(rows, "dp", axis=0, tiled=True)
+    return collect_2(rows, "dp", 0)
 
 
 def sum_rows(terms):

time: 3390 us -> 3890 us (1.15)
  waiting for transfers between devices: 2530 us -> 2970 us
  other arithmetic: 101 us -> 148 us
    ppermute x0 -> x6, waiting for transfers between devices: none -> 1240 us  [collect_2(): theirs = lax.ppermute(grown, axis, [(d, d ^ reach) for d in range(ways)])]
    all_gather x2 -> x0, waiting for transfers between devices: 799 us -> none  [spread_rows(): return lax.all_gather(rows, 'dp', axis=0, tiled=True)]
    select_n x0 -> x4, other arithmetic: none -> 46.3 us  [collect_2(): grown = jnp.where(here & reach == 0, mine_first, theirs_first)]
  transfers between devices with their start and end apart: 20 -> 24, of which waited for: 18 -> 22; matrix products, arithmetic and copies ran while one was open for 9% -> 8% of each run, Pallas kernels for 0% -> 0%
where the time goes in v1:
time: 3890 us; the launch traced here: 3880 us
  waiting for transfers between devices  2970 us (76%)
  matrix products  519 us (13%)
  other arithmetic  148 us (4%)
  blocking collectives  126 us (3%)
  local copies, waits for them, and re-layouts  71.4 us (2%)
    ppermute x6, waiting for transfers between devices, collect_2(): theirs = lax.ppermute(grown, axis, [(d, d ^ reach) for d in range(ways)])  1240 us
    reduce_scatter x2, waiting for transfers between devices, sum_rows(): lax.psum_scatter(terms.astype(jnp.bfloat16), 'dp', scatter_dimension=0, t...  685 us
    all_gather x1, waiting for transfers between devices, per_device(): lax.all_gather(keyvalue_weight, 'dp', axis=0, tiled=True)  230 us
    reduce_scatter x1, waiting for transfers between devices, per_device(): lax.psum_scatter(grad_projection.astype(jnp.bfloat16), 'dp', scatter_dime...  152 us
    reduce_scatter x1, waiting for transfers between devices, per_device(): lax.psum_scatter(grad_query.astype(jnp.bfloat16), 'dp', scatter_dimension...  149 us
    all_to_all x1, waiting for transfers between devices, per_device(): lax.all_to_all(keyvalue_terms.astype(jnp.bfloat16), 'expert', split_axis=...  90.5 us
    reduce_scatter x1, waiting for transfers between devices, per_device(): lax.psum_scatter(grad_keyvalue.astype(jnp.bfloat16), 'dp', scatter_dimens...  82 us
  transfers between devices with their start and end apart: 24, of which 22 were waited for; matrix products, arithmetic and copies ran while one was open for 8% of the time, Pallas kernels for 0%

profile of v1, /device:TPU:0, one launch (start us, length us, event | category | flops | bytes accessed | tf_op | source)
XLA Modules:
  0.0 3884.0 jit_solution(10468117140742765973)
XLA Ops:
  10.3 230.2 %all-gather.7.cloned.1.call-done = bf16[2048,4096]{1,0:T(8,128)(2,1)} async-done(((bf16[256,4096]{1,0:T(8,128)(2,1)}), bf16[2048,4096]{1,0:T(8,128)(2,1)}) %all-gather.7.cloned.1.call-update) | async-done | bytes 16777232 | tf_op jit(solution)/shard_map/all_gather | solution.py:141
  303.1 62.7 %all-gather.11.cloned.1.call-done = bf16[1,2048,2048]{2,1,0:T(8,128)(2,1)} async-done(((bf16[1,256,2048]{2,1,0:T(8,128)(2,1)}), bf16[1,2048,2048]{2,1,0:T(8,128)(2,1)}) %all-gather.11.cloned.1.call-update) | async-done | bytes 8388624 | tf_op jit(solution)/shard_map/all_gather | solution.py:143
  381.0 43.4 %all-gather.9.cloned.1.call-done = bf16[1024,4096]{1,0:T(8,128)(2,1)} async-done(((bf16[256,4096]{1,0:T(8,128)(2,1)}), bf16[1024,4096]{1,0:T(8,128)(2,1)}) %all-gather.9.cloned.1.call-update) | async-done | bytes 8388624 | tf_op jit(solution)/shard_map/all_gather | solution.py:153
  498.4 53.0 %all-gather.13.cloned.1.call-done = bf16[1,2048,2048]{2,1,0:T(8,128)(2,1)} async-done(((bf16[1,256,2048]{2,1,0:T(8,128)(2,1)}), bf16[1,2048,2048]{2,1,0:T(8,128)(2,1)}) %all-gather.13.cloned.1.call-update) | async-done | bytes 8388624 | tf_op jit(solution)/shard_map/all_gather | solution.py:144
  607.4 35.0 all_to_all.45
  642.5 58.5 %collective-permute-done = bf16[640,2048]{1,0:T(8,128)(2,1)} collective-permute-done((bf16[640,2048]{1,0:T(8,128)(2,1)}, bf16[640,2048]{1,0:T(8,128)(2,1)}, u32[]{:S(2)}, u32[]{:S(2)}) %collective-permute-start) | collective-permute-done | bytes 2621472 | tf_op jit(solution)/shard_map/ppermute | solution.py:19
  708.1 113.8 %collective-permute-done.1 = bf16[1280,2048]{1,0:T(8,128)(2,1)} collective-permute-done((bf16[1280,2048]{1,0:T(8,128)(2,1)}, bf16[1280,2048]{1,0:T(8,128)(2,1)}, u32[]{:S(2)}, u32[]{:S(2)}) %collective-permute-start.1) | collective-permute-done | bytes 5242912 | tf_op jit(solution)/shard_map/ppermute | solution.py:19
  835.2 450.8 %collective-permute-done.2 = bf16[2560,2048]{1,0:T(8,128)(2,1)} collective-permute-done((bf16[2560,2048]{1,0:T(8,128)(2,1)}, bf16[2560,2048]{1,0:T(8,128)(2,1)}, u32[]{:S(2)}, u32[]{:S(2)}) %collective-permute-start.2) | collective-permute-done | bytes 10485792 | tf_op jit(solution)/shard_map/ppermute | solution.py:19
  1313.4 33.1 multiply_convert_fusion.3
  1369.6 341.8 %reduce-scatter.7.cloned.1.call-done = bf16[640,2048]{1,0:T(8,128)(2,1)} async-done(((bf16[5120,2048]{1,0:T(8,128)(2,1)}), bf16[640,2048]{1,0:T(8,128)(2,1)}) %reduce-scatter.7.cloned.1.call-update) | async-done | bytes 2621456 | tf_op jit(solution)/shard_map/reduce_scatter | solution.py:104
  1758.9 34.0 all_to_all.46
  1794.4 56.8 %collective-permute-done.3 = bf16[640,2048]{1,0:T(8,128)(2,1)S(1)} collective-permute-done((bf16[640,2048]{1,0:T(8,128)(2,1)S(1)}, bf16[640,2048]{1,0:T(8,128)(2,1)S(1)}, u32[]{:S(2)}, u32[]{:S(2)}) %collective-permute-start.3) | collective-permute-done | bytes 2621472 | tf_op jit(solution)/shard_map/ppermute | solution.py:19
  1859.1 113.4 %collective-permute-done.4 = bf16[1280,2048]{1,0:T(8,128)(2,1)S(1)} collective-permute-done((bf16[1280,2048]{1,0:T(8,128)(2,1)S(1)}, bf16[1280,2048]{1,0:T(8,128)(2,1)S(1)}, u32[]{:S(2)}, u32[]{:S(2)}) %collective-permute-start.4) | collective-permute-done | bytes 5242912 | tf_op jit(solution)/shard_map/ppermute | solution.py:19
  1996.3 448.9 %collective-permute-done.5 = bf16[2560,2048]{1,0:T(8,128)(2,1)S(1)} collective-permute-done((bf16[2560,2048]{1,0:T(8,128)(2,1)S(1)}, bf16[2560,2048]{1,0:T(8,128)(2,1)S(1)}, u32[]{:S(2)}, u32[]{:S(2)}) %collective-permute-start.5) | collective-permute-done | bytes 10485792 | tf_op jit(solution)/shard_map/ppermute | solution.py:19
  2449.1 35.2 multiply_convert_fusion.1
  2540.5 343.0 %reduce-scatter.9.cloned.1.call-done = bf16[640,2048]{1,0:T(8,128)(2,1)} async-done(((bf16[5120,2048]{1,0:T(8,128)(2,1)}), bf16[640,2048]{1,0:T(8,128)(2,1)}) %reduce-scatter.9.cloned.1.call-update) | async-done | bytes 2621456 | tf_op jit(solution)/shard_map/reduce_scatter | solution.py:104
  2940.2 31.2 all-to-all-done.6
  3004.4 35.8 multiply_reduce_fusion
  3052.8 34.6 multiply_convert_fusion
  3128.2 90.5 %all-to-all-done.8 = bf16[4,256,4096]{1,2,0:T(8,128)(2,1)} async-done(((bf16[4,256,4096]{1,2,0:T(8,128)(2,1)}), bf16[4,256,4096]{1,2,0:T(8,128)(2,1)}, u32[]{:S(2)}, u32[]{:S(2)}) %all-to-all-start.8) | async-done | bytes 8388640 | tf_op jit(solution)/shard_map/all_to_all | solution.py:280
  3434.6 82.0 %reduce-scatter.11.cloned.1.call-done = bf16[256,4096]{1,0:T(8,128)(2,1)} async-done(((bf16[2048,4096]{1,0:T(8,128)(2,1)}), bf16[256,4096]{1,0:T(8,128)(2,1)}) %reduce-scatter.11.cloned.1.call-update) | async-done | bytes 2097168 | tf_op jit(solution)/shard_map/reduce_scatter | solution.py:305
  3516.6 152.1 %reduce-scatter.17.cloned.1.call-done = bf16[256,2048]{1,0:T(8,128)(2,1)} async-done(((bf16[2048,2048]{1,0:T(8,128)(2,1)}), bf16[256,2048]{1,0:T(8,128)(2,1)}) %reduce-scatter.17.cloned.1.call-update) | async-done | bytes 1048592 | tf_op jit(solution)/shard_map/reduce_scatter | solution.py:314
  3671.5 148.7 %reduce-scatter.15.cloned.1.call-done = bf16[256,2048]{1,0:T(8,128)(2,1)} async-done(((bf16[2048,2048]{1,0:T(8,128)(2,1)}), bf16[256,2048]{1,0:T(8,128)(2,1)}) %reduce-scatter.15.cloned.1.call-update) | async-done | bytes 1048592 | tf_op jit(solution)/shard_map/reduce_scatter | solution.py:311
  3823.1 50.1 %all-reduce.6.cloned.1.call-done = bf16[256,4096]{1,0:T(8,128)(2,1)} async-done(((bf16[256,4096]{1,0:T(8,128)(2,1)}), bf16[256,4096]{1,0:T(8,128)(2,1)}) %all-reduce.6.cloned.1.call-update) | async-done | bytes 2097168 | tf_op jit(solution)/shard_map/psum | solution.py:325
  (324 shorter events, 788.7 us)
Async XLA Ops:
  7.2 233.3 %all-gather.7.cloned.1.call-start = ((), (), s32[]{:S(2)}) async-start(), calls=%async_computation.15 | async-start | bytes 18874368 | tf_op jit(solution)/shard_map/all_gather | solution.py:141
  7.9 357.8 %all-gather.11.cloned.1.call-start = ((), (), s32[]{:S(2)}) async-start(), calls=%async_computation.24 | async-start | bytes 9437184 | tf_op jit(solution)/shard_map/all_gather | solution.py:143
  8.7 415.7 %all-gather.9.cloned.1.call-start = ((), (), s32[]{:S(2)}) async-start(), calls=%async_computation.16 | async-start | bytes 10485760 | tf_op jit(solution)/shard_map/all_gather | solution.py:153
  267.2 36.0 all-to-all-start
  271.7 279.7 %all-gather.13.cloned.1.call-start = ((), (), s32[]{:S(2)}) async-start(), calls=%async_computation.25 | async-start | bytes 9437184 | tf_op jit(solution)/shard_map/all_gather | solution.py:144
  561.4 37.8 all-to-all-start.1
  566.1 1145.3 %reduce-scatter.7.cloned.1.call-start = ((), (), s32[]{:S(2)}) async-start(), calls=%async_computation.17 | async-start | bytes 23592960 | tf_op jit(solution)/shard_map/reduce_scatter | solution.py:104
  642.4 58.6 %collective-permute-start = (bf16[640,2048]{1,0:T(8,128)(2,1)}, bf16[640,2048]{1,0:T(8,128)(2,1)}, u32[]{:S(2)}, u32[]{:S(2)}) collective-permute-start(bf16[640,2048]{1,0:T(8,128)(2,1)} %bitcast.30), channel_id=1, source_target_pairs={{0,4},{4,0},{8,12},{12,8},{16,20},{20,16},{24,28},{28,24},{1,5},{5... | collective-permute-start | bytes 7864328 | tf_op jit(solution)/shard_map/ppermute | solution.py:19
  708.1 113.8 %collective-permute-start.1 = (bf16[1280,2048]{1,0:T(8,128)(2,1)}, bf16[1280,2048]{1,0:T(8,128)(2,1)}, u32[]{:S(2)}, u32[]{:S(2)}) collective-permute-start(bf16[1280,2048]{1,0:T(8,128)(2,1)} %maximum_select_fusion.4), channel_id=1, source_target_pairs={{0,8},{4,12},{8,0},{12,4},{16,24},{20,28},{24,16},{28,20},{1,9},{5... | collective-permute-start | bytes 15728648 | tf_op jit(solution)/shard_map/ppermute | solution.py:19
  835.2 450.8 %collective-permute-start.2 = (bf16[2560,2048]{1,0:T(8,128)(2,1)}, bf16[2560,2048]{1,0:T(8,128)(2,1)}, u32[]{:S(2)}, u32[]{:S(2)}) collective-permute-start(bf16[2560,2048]{1,0:T(8,128)(2,1)} %maximum_select_fusion.2), channel_id=1, source_target_pairs={{0,16},{4,20},{8,24},{12,28},{16,0},{20,4},{24,8},{28,12},{1,17},{... | collective-permute-start | bytes 31457288 | tf_op jit(solution)/shard_map/ppermute | solution.py:19
  1711.4 35.9 all-to-all-start.3
  1716.0 1167.6 %reduce-scatter.9.cloned.1.call-start = ((), (), s32[]{:S(2)}) async-start(), calls=%async_computation.18 | async-start | bytes 23592960 | tf_op jit(solution)/shard_map/reduce_scatter | solution.py:104
  1792.9 58.2 %collective-permute-start.3 = (bf16[640,2048]{1,0:T(8,128)(2,1)S(1)}, bf16[640,2048]{1,0:T(8,128)(2,1)S(1)}, u32[]{:S(2)}, u32[]{:S(2)}) collective-permute-start(bf16[640,2048]{1,0:T(8,128)(2,1)S(1)} %bitcast.241), channel_id=1, source_target_pairs={{0,4},{4,0},{8,12},{12,8},{16,20},{20,16},{24,28},{28,24},{1,5},{5... | collective-permute-start | bytes 7864328 | tf_op jit(solution)/shard_map/ppermute | solution.py:19
  1858.9 113.6 %collective-permute-start.4 = (bf16[1280,2048]{1,0:T(8,128)(2,1)S(1)}, bf16[1280,2048]{1,0:T(8,128)(2,1)S(1)}, u32[]{:S(2)}, u32[]{:S(2)}) collective-permute-start(bf16[1280,2048]{1,0:T(8,128)(2,1)S(1)} %maximum_select_fusion.5), channel_id=1, source_target_pairs={{0,8},{4,12},{8,0},{12,4},{16,24},{20,28},{24,16},{28,20},{1,9},{5... | collective-permute-start | bytes 15728648 | tf_op jit(solution)/shard_map/ppermute | solution.py:19
  1994.7 450.5 %collective-permute-start.5 = (bf16[2560,2048]{1,0:T(8,128)(2,1)S(1)}, bf16[2560,2048]{1,0:T(8,128)(2,1)S(1)}, u32[]{:S(2)}, u32[]{:S(2)}) collective-permute-start(bf16[2560,2048]{1,0:T(8,128)(2,1)S(1)} %maximum_select_fusion.3), channel_id=1, source_target_pairs={{0,16},{4,20},{8,24},{12,28},{16,0},{20,4},{24,8},{28,12},{1,17},{... | collective-permute-start | bytes 31457288 | tf_op jit(solution)/shard_map/ppermute | solution.py:19
  2883.6 36.1 all-to-all-start.5
  2936.3 35.2 all-to-all-start.6
  3119.8 99.0 %all-to-all-start.8 = ((bf16[4,256,4096]{1,2,0:T(8,128)(2,1)}), bf16[4,256,4096]{1,2,0:T(8,128)(2,1)}, u32[]{:S(2)}, u32[]{:S(2)}) async-start(bf16[4,256,4096]{1,2,0:T(8,128)(2,1)} %pad_maximum_fusion), calls=%async_computation.10 | async-start | bytes 16777216 | tf_op jit(solution)/shard_map/all_to_all | solution.py:280
  3125.6 295.8 %reduce-scatter.13.cloned.1.call-start = ((), (), s32[]{:S(2)}) async-start(), calls=%async_computation.21 | async-start | bytes 36864 | tf_op jit(solution)/shard_map/reduce_scatter | solution.py:308
  3128.2 388.4 %reduce-scatter.11.cloned.1.call-start = ((), (), s32[]{:S(2)}) async-start(), calls=%async_computation.19 | async-start | bytes 18874368 | tf_op jit(solution)/shard_map/reduce_scatter | solution.py:305
  3235.2 433.5 %reduce-scatter.17.cloned.1.call-start = ((), (), s32[]{:S(2)}) async-start(), calls=%async_computation.23 | async-start | bytes 9437184 | tf_op jit(solution)/shard_map/reduce_scatter | solution.py:314
  3247.9 572.4 %reduce-scatter.15.cloned.1.call-start = ((), (), s32[]{:S(2)}) async-start(), calls=%async_computation.22 | async-start | bytes 9437184 | tf_op jit(solution)/shard_map/reduce_scatter | solution.py:311
  3344.3 34.9 all-to-all-start.7
  3348.0 525.1 %all-reduce.6.cloned.1.call-start = ((), (), s32[]{:S(2)}) async-start(), calls=%async_computation.20 | async-start | bytes 4194304 | tf_op jit(solution)/shard_map/psum | solution.py:325
  (78 other events, 9561.2 us)
Sparse Core Ops, SparseCore 0:
  10.2 230.2 all-gather.6
  242.6 123.1 all-gather.10
  367.9 56.4 all-gather.8
  426.4 124.9 all-gather.12
  1369.7 341.6 reduce-scatter.6
  2540.6 342.9 reduce-scatter.8
  3129.6 53.1 reduce-scatter.12
  3235.4 281.1 reduce-scatter.10
  3520.7 148.0 reduce-scatter.16
  3672.2 147.9 reduce-scatter.14
  3822.8 50.3 all-reduce.5
